TPU v7x, 256 devices: a whole 4x4x8 slice. The times are simulated.
256 devices in a mesh: seq: 32 (over y, z), tp: 8 (over x, core).
Axes of the slice: x: 4, y: 4, z: 8, core: 2. Of those that a mesh axis runs over, the one named last changes fastest.
Arguments:
- tokens: bfloat16 [16384, 4096], P('seq', 'tp'), may hold values from -40 to 40, as said below
- w_query: bfloat16 [4096, 2048], P(None, 'tp'), may hold values from -0.09375 to 0.09375
- w_key: bfloat16 [4096, 2048], P(None, 'tp'), may hold values from -0.09375 to 0.09375
- w_value: bfloat16 [4096, 2048], P(None, 'tp'), may hold values from -0.09375 to 0.09375
- w_gate: bfloat16 [4096, 2048], P(None, 'tp'), may hold values from -0.09375 to 0.09375
- w_out: bfloat16 [2048, 4096], P(None, 'tp'), may hold values from -0.125 to 0.125
- decay_rate: float32 [16], replicated, may hold values from 1.8310547e-05 to 0.0333333333, as said below
- state_in: float32 [16, 128, 128], P('tp'), may hold values from -192 to 192
Outputs:
- layer_out: bfloat16 [16384, 4096], P('seq', 'tp')
Inputs may be any that keep to these rules, and one draw needn't show every extreme that they name: tokens have scales that vary by row and by column. `decay_rate`: each head either forgets within a few tens of positions or keeps its state over the whole slab.
All inputs are finite; a program needn't handle non-finite values.
Results may differ from a plain program's by a relative error of at most 0.0033.
Values may be sent and summed in bfloat16 or wider, within the bound.
A program may use at most 64 MiB of HBM per device.

v0:
```python
import jax
import jax.numpy as jnp
from jax import lax
from jax.sharding import PartitionSpec as P


def per_device(tokens, w_query, w_key, w_value, w_gate, w_out, decay_rate, state_in):
    hi = lax.Precision.HIGHEST
    row_count = tokens.shape[0]
    width_all = w_query.shape[0]
    heads_here = state_in.shape[0]
    head_dim = state_in.shape[1]
    tp_index = lax.axis_index("tp")
    seq_index = lax.axis_index("seq")
    weight_set = (w_query, w_key, w_value, w_gate)
    gathered = lax.all_gather(tokens, "tp", axis=1, tiled=True)
    gathered_f = gathered.astype(jnp.float32)
    square_sum = jnp.sum(gathered_f * gathered_f, axis=1, keepdims=True)
    raw_set = tuple(
        (jnp.dot(gathered, weight, preferred_element_type=jnp.float32) for weight in weight_set)
    )
    inv_rms = lax.rsqrt(square_sum / float(width_all) + 1e-06)

    def to_heads(array):
        return array.reshape(row_count, heads_here, head_dim).transpose(1, 0, 2)

    query_h = to_heads(jax.nn.silu(raw_set[0] * inv_rms).astype(jnp.bfloat16))
    key_h = to_heads(jax.nn.silu(raw_set[1] * inv_rms).astype(jnp.bfloat16))
    value_h = to_heads((raw_set[2] * inv_rms).astype(jnp.bfloat16))
    gate = jax.nn.silu(raw_set[3] * inv_rms)
    rate_here = lax.dynamic_slice_in_dim(decay_rate, tp_index * heads_here, heads_here)
    rate_col = rate_here[:, None]
    positions = jnp.arange(row_count).astype(jnp.float32)
    lower = positions[:, None] >= positions[None, :]
    gap_mask = jnp.where(lower, positions[:, None] - positions[None, :], 0.0)
    scores = jnp.einsum("hid,hjd->hij", query_h, key_h, preferred_element_type=jnp.float32)
    mask = jnp.where(lower[None], jnp.exp(-rate_col[:, :, None] * gap_mask[None]), 0.0)
    weights = (scores * mask).astype(jnp.bfloat16)
    intra = jnp.einsum("hij,hje->hie", weights, value_h, preferred_element_type=jnp.float32)
    value_f = value_h.astype(jnp.float32)
    tail_decay = jnp.exp(-rate_col * (row_count - 1.0 - positions[None, :]))
    local_state = jnp.einsum(
        "hid,hie->hde", key_h.astype(jnp.float32) * tail_decay[:, :, None], value_f, precision=hi
    )
    piece = lax.all_gather(
        local_state[None].astype(jnp.bfloat16), "seq", axis=0, tiled=True
    ).astype(jnp.float32)
    count = piece.shape[0]
    source = jnp.arange(count)
    distance = seq_index - 1 - source
    exponent = (row_count * jnp.maximum(distance, 0)).astype(jnp.float32)
    factor = jnp.where(
        distance[:, None] >= 0, jnp.exp(-rate_here[None, :] * exponent[:, None]), 0.0
    )
    prefix = jnp.zeros_like(local_state) + jnp.sum(factor[:, :, None, None] * piece, axis=0)
    offset = (row_count * seq_index).astype(jnp.float32)
    incoming = prefix + jnp.exp(-rate_here * offset)[:, None, None] * state_in
    lead_decay = jnp.exp(-rate_col * (positions[None, :] + 1.0))
    inter = jnp.einsum(
        "hid,hde->hie", query_h.astype(jnp.float32) * lead_decay[:, :, None], incoming, precision=hi
    )
    attended = intra + inter
    norm_inv = lax.rsqrt(jnp.mean(attended * attended, axis=2, keepdims=True) + 1e-06)
    normed = (attended * norm_inv).transpose(1, 0, 2).reshape(row_count, heads_here * head_dim)
    hidden = (normed * gate).astype(jnp.bfloat16)
    branch = jnp.dot(
        lax.all_gather(hidden, "tp", axis=1, tiled=True), w_out, preferred_element_type=jnp.float32
    )
    return (tokens.astype(jnp.float32) + branch).astype(jnp.bfloat16)


def solution(mesh):
    return jax.shard_map(
        per_device,
        mesh=mesh,
        in_specs=(
            P("seq", "tp"),
            P(None, "tp"),
            P(None, "tp"),
            P(None, "tp"),
            P(None, "tp"),
            P(None, "tp"),
            P(),
            P("tp", None, None),
        ),
        out_specs=P("seq", "tp"),
        check_vma=False,
    )
```

profile of v0, /device:TPU:1, one launch (start us, length us, event | category | flops | bytes accessed | tf_op | source)
XLA Modules:
  0.0 186.8 jit_solution(16274440902370304356)
XLA Ops:
  6.5 0.0 copy-start
  6.5 0.0 all-gather.5.cloned.1.call-start
  6.5 0.7 all-gather.5.cloned.1.call-update
  7.3 0.0 all-gather.9.cloned.1.call-start
  7.3 1.3 multiply_exponential_fusion.2
  8.6 0.0 copy-start.7
  8.6 0.7 multiply_exponential_fusion
  9.3 38.8 %all-gather.5.cloned.1.call-done = bf16[512,4096]{1,0:T(8,128)(2,1)} async-done(((bf16[512,512]{1,0:T(8,128)(2,1)}), bf16[512,4096]{1,0:T(8,128)(2,1)}) %all-gather.5.cloned.1.call-update) | async-done | bytes 4194320 | tf_op jit(solution)/shard_map/all_gather | solution.py:16
  48.1 0.0 copy-start.1
  48.1 3.2 %multiply_reduce_fusion = f32[512]{0:T(512)S(1)} fusion(bf16[512,4096]{1,0:T(8,128)(2,1)} %all-gather.5.cloned.1.call-done), kind=kLoop, calls=%fused_computation | loop fusion | flops 6290944 | bytes 4196352 | tf_op jit(solution)/shard_map/reduce_sum | solution.py:18
  51.3 0.2 copy-done.1
  51.5 0.0 copy-start.9
  51.5 2.9 %fusion.4 = bf16[512,256]{0,1:T(8,128)(2,1)S(1)} fusion(bf16[512,4096]{1,0:T(8,128)(2,1)S(1)} %copy-done.1, bf16[4096,256]{1,0:T(8,128)(2,1)} %param.11, f32[512]{0:T(512)S(1)} %add_rsqrt_fusion), kind=kOutput, calls=%fused_computation.12 | convolution fusion | flops 1074003968 | bytes 6555648 | tf_op jit(solution)/shard_map/dot_general | solution.py:20
  54.5 0.0 copy-start.4
  54.5 0.2 copy.15
  54.6 4.2 %multiply_convert_fusion.1 = bf16[512,256]{0,1:T(8,128)(2,1)S(1)} fusion(bf16[512,4096]{1,0:T(8,128)(2,1)} %all-gather.5.cloned.1.call-done, bf16[4096,256]{1,0:T(8,128)(2,1)} %param.10, f32[512]{0:T(512)S(1)} %add_rsqrt_fusion), kind=kOutput, calls=%fused_computation.29 | convolution fusion | flops 1074528256 | bytes 6555648 | tf_op jit(solution)/shard_map/dot_general | solution.py:20
  58.9 0.0 copy-done.4
  58.9 0.0 copy-start.3
  58.9 0.7 copy-done.3
  59.6 1.0 convolution_convert_fusion
  60.6 0.0 all-gather.9.cloned.1.call-update
  60.7 0.0 all-gather.7.cloned.1.call-start
  60.8 0.0 copy-done.7
  60.8 0.1 exponential_select_fusion
  60.9 0.9 broadcast_compare_fusion
  61.8 0.2 subtract_select_fusion
  62.0 0.0 copy-done.9
  62.0 5.0 %multiply_convert_fusion.2 = bf16[512,256]{0,1:T(8,128)(2,1)} fusion(bf16[512,4096]{1,0:T(8,128)(2,1)} %all-gather.5.cloned.1.call-done, bf16[4096,256]{1,0:T(8,128)(2,1)} %param.9, f32[512]{0:T(512)S(1)} %add_rsqrt_fusion), kind=kOutput, calls=%fused_computation.30 | convolution fusion | flops 1074528256 | bytes 6555648 | tf_op jit(solution)/shard_map/dot_general | solution.py:20
  66.9 0.0 copy-start.5
  66.9 1.2 copy.14
  68.1 66.4 %all-gather.9.cloned.1.call-done = bf16[64,128,128]{2,1,0:T(8,128)(2,1)} async-done(((bf16[2,128,128]{2,1,0:T(8,128)(2,1)}), bf16[64,128,128]{2,1,0:T(8,128)(2,1)}) %all-gather.9.cloned.1.call-update) | async-done | bytes 2097168 | tf_op jit(solution)/shard_map/all_gather | solution.py:45
  134.4 0.0 copy-start.6
  134.4 0.0 copy-start.8
  134.5 2.1 %fusion = f32[2,128,128]{2,1,0:T(8,128)S(1)} fusion(bf16[32,2,128,128]{3,2,1,0:T(8,128)(2,1)} %bitcast.42, f32[32,2]{1,0:T(8,128)S(1)} %exponential_select_fusion), kind=kLoop, calls=%fused_computation.2 | loop fusion | flops 3112960 | bytes 2228480 | tf_op jit(solution)/shard_map/reduce_sum | solution.py:55
  136.5 0.0 copy-done.5
  136.5 0.0 copy-done.6
  136.5 0.0 copy-done.8
  136.6 1.6 fusion.12
  138.1 0.0 copy-start.10
  138.1 3.0 %multiply_reduce_fusion.1 = (f32[2,512]{1,0:T(2,128)S(1)}, f32[2,512,128]{1,2,0:T(8,128)}) fusion(f32[2,512,128]{1,2,0:T(8,128)} %fusion.12, bf16[2,512,128]{1,2,0:T(8,128)(2,1)} %bitcast.46, bf16[2,512,128]{1,2,0:T(8,128)(2,1)} %bitcast.44, f32[512,512]{1,0:T(8,128)S(1)} %subtract_select_fusion, f32[2]{0:T(128)} %copy-done.7, ...), kind=kOutput, calls=%fused_computation.22 | convolution fusion | flops 270924800 | bytes 3149832 | tf_op jit(solution)/shard_map/hij,hje->hie/dot_general | solution.py:39
  141.1 1.1 bitcast_multiply_fusion.1
  142.2 0.0 copy-done.10
  142.2 0.0 copy-start.2
  142.3 5.0 %fusion.9 = bf16[512,256]{0,1:T(8,128)(2,1)} fusion(f32[512,2,128]{0,2,1:T(8,128)S(1)} %bitcast_multiply_fusion.1, bf16[512,4096]{1,0:T(8,128)(2,1)} %all-gather.5.cloned.1.call-done, bf16[4096,256]{1,0:T(8,128)(2,1)} %param.12, f32[512]{0:T(512)S(1)} %copy-done.10), kind=kOutput, calls=%fused_computation.20 | convolution fusion | flops 1074659328 | bytes 7079936 | tf_op jit(solution)/shard_map/dot_general | solution.py:20
  147.3 0.0 all-gather.7.cloned.1.call-update
  147.3 29.4 %all-gather.7.cloned.1.call-done = bf16[512,2048]{0,1:T(8,128)(2,1)} async-done(((bf16[512,256]{0,1:T(8,128)(2,1)}), bf16[512,2048]{0,1:T(8,128)(2,1)}) %all-gather.7.cloned.1.call-update) | async-done | bytes 2097168 | tf_op jit(solution)/shard_map/all_gather | solution.py:67
  176.6 0.0 copy-done
  176.6 0.0 copy-done.2
  176.6 3.7 %fusion.2 = bf16[512,512]{1,0:T(8,128)(2,1)} fusion(bf16[512,2048]{0,1:T(8,128)(2,1)} %all-gather.7.cloned.1.call-done, bf16[2048,512]{1,0:T(8,128)(2,1)S(1)} %copy-done, bf16[512,512]{1,0:T(8,128)(2,1)S(1)} %copy-done.2), kind=kOutput, calls=%fused_computation.6 | convolution fusion | flops 1074528256 | bytes 5242880 | tf_op jit(solution)/shard_map/dot_general | solution.py:66
  (6 shorter events, 0.0 us)
Async XLA Ops:
  6.5 170.1 %copy-start = (bf16[2048,512]{1,0:T(8,128)(2,1)S(1)}, bf16[2048,512]{1,0:T(8,128)(2,1)}, u32[]{:S(2)}) copy-start(bf16[2048,512]{1,0:T(8,128)(2,1)} %param.13) | copy-start | bytes 6291460
  6.5 41.5 %all-gather.5.cloned.1.call-start = ((), (), s32[]{:S(2)}) async-start(), calls=%async_computation | async-start | bytes 4718592 | tf_op jit(solution)/shard_map/all_gather | solution.py:16
  7.3 127.2 %all-gather.9.cloned.1.call-start = ((), (), s32[]{:S(2)}) async-start(), calls=%async_computation.2 | async-start | bytes 2162688 | tf_op jit(solution)/shard_map/all_gather | solution.py:45
  8.6 52.2 %copy-start.7 = (f32[2]{0:T(128)}, f32[2]{0:T(128)S(1)}, u32[]{:S(2)}) copy-start(f32[2]{0:T(128)S(1)} %get-tuple-element.6) | copy-start | bytes 28
  48.1 3.4 %copy-start.1 = (bf16[512,4096]{1,0:T(8,128)(2,1)S(1)}, bf16[512,4096]{1,0:T(8,128)(2,1)}, u32[]{:S(2)}) copy-start(bf16[512,4096]{1,0:T(8,128)(2,1)} %all-gather.5.cloned.1.call-done) | copy-start | bytes 12582916
  51.5 10.4 %copy-start.9 = (f32[512]{0:T(512)}, f32[512]{0:T(512)S(1)}, u32[]{:S(2)}) copy-start(f32[512]{0:T(512)S(1)} %add_rsqrt_fusion) | copy-start | bytes 6148
  54.5 4.4 %copy-start.4 = (bf16[512,256]{0,1:T(8,128)(2,1)}, bf16[512,256]{0,1:T(8,128)(2,1)S(1)}, u32[]{:S(2)}) copy-start(bf16[512,256]{0,1:T(8,128)(2,1)S(1)} %fusion.4) | copy-start | bytes 786436
  58.9 0.7 copy-start.3
  60.7 116.0 %all-gather.7.cloned.1.call-start = ((), (), s32[]{:S(2)}) async-start(), calls=%async_computation.1 | async-start | bytes 2359296 | tf_op jit(solution)/shard_map/all_gather | solution.py:67
  66.9 69.6 %copy-start.5 = (f32[2,128,128]{2,1,0:T(8,128)S(1)}, f32[2,128,128]{2,1,0:T(8,128)}, u32[]{:S(2)}) copy-start(f32[2,128,128]{2,1,0:T(8,128)} %param.15) | copy-start | bytes 393220
  134.4 2.1 %copy-start.6 = (f32[2,512]{1,0:T(2,128)S(1)}, f32[2,512]{1,0:T(2,128)}, u32[]{:S(2)}) copy-start(f32[2,512]{1,0:T(2,128)} %get-tuple-element.8) | copy-start | bytes 12292
  134.4 2.1 %copy-start.8 = (f32[2]{0:T(128)S(1)}, f32[2]{0:T(128)}, u32[]{:S(2)}) copy-start(f32[2]{0:T(128)} %get-tuple-element.5) | copy-start | bytes 28
  138.1 4.1 %copy-start.10 = (f32[512]{0:T(512)S(1)}, f32[512]{0:T(512)}, u32[]{:S(2)}) copy-start(f32[512]{0:T(512)} %copy-done.9) | copy-start | bytes 6148
  142.2 34.4 %copy-start.2 = (bf16[512,512]{1,0:T(8,128)(2,1)S(1)}, bf16[512,512]{1,0:T(8,128)(2,1)}, u32[]{:S(2)}) copy-start(bf16[512,512]{1,0:T(8,128)(2,1)} %param.8) | copy-start | bytes 1572868
Sparse Core Ops, SparseCore 0:
  9.2 38.8 all-gather.4
  60.8 73.6 all-gather.8
  147.4 29.1 all-gather.6
where the time goes:
time: 187 us
  waiting for transfers between devices  135 us (72%)
  matrix products  26.3 us (14%)
  between operations  13.3 us (7%)
  other arithmetic  9.55 us (5%)
  local copies, waits for them, and re-layouts  2.27 us (1%)
    all_gather x1, waiting for transfers between devices, per_device(): lax.all_gather(local_state[None].astype(jnp.bfloat16), 'seq', axis=0, til...  66.4 us
    all_gather x1, waiting for transfers between devices, per_device(): gathered = lax.all_gather(tokens, 'tp', axis=1, tiled=True)  38.8 us
    all_gather x1, waiting for transfers between devices, per_device(): lax.all_gather(hidden, 'tp', axis=1, tiled=True)  29.4 us
    dot_general x4, matrix products, per_device(): jnp.dot(gathered, weight, preferred_element_type=jnp.float32)  17.1 us
  transfers between devices with their start and end apart: 3, of which 3 were waited for; matrix products, arithmetic and copies ran while one was open for 5% of the time, Pallas kernels for 0%

commit v1 on v0

v1 whole, which is shorter than its diff:
```python
import jax
import jax.numpy as jnp
from jax import lax
from jax.experimental import pallas as pl
from jax.experimental.pallas import tpu as pltpu
from jax.sharding import PartitionSpec as P

NX, NY, NZ = 4, 4, 8
ROWS = 512
WIDTH = 4096
HD = 128
CH = 256
BF = jnp.bfloat16
F32 = jnp.float32


def silu(z):
    return z / (1.0 + jnp.exp(-z))


def kernel(tok_in, wq, wk, wv, wg, wo, rate_ref, st_in, out_ref,
           tok, w, wov, stv, acc, sq, mask, tail, lead, kb, vb, qb, gate, intra,
           lsend, r1, rtsend, rt, ssend, srecv, hid, oacc,
           load_sem, tok_send, tok_recv, s1s, s1r, s2s, s2r, s3s, s3r, hid_send, hid_recv):
    tp = lax.axis_index("tp")
    seq = lax.axis_index("seq")
    x, core = tp // 2, tp % 2
    y, z = seq // NZ, seq % NZ
    xr, xl, xo = (x + 1) % NX, (x + 3) % NX, (x + 2) % NX
    right, left = (seq, 2 * xr + core), (seq, 2 * xl + core)
    partner = (seq, 2 * x + 1 - core)
    mine, other = core, 1 - core

    def signal(dev):
        pl.semaphore_signal(barrier, inc=1, device_id=dev, device_id_type=pl.DeviceIdType.MESH)

    def remote(src, dst, ss, rs, dev):
        return pltpu.make_async_remote_copy(
            src_ref=src, dst_ref=dst, send_sem=ss, recv_sem=rs, device_id=dev,
            device_id_type=pl.DeviceIdType.MESH)

    loads = []
    for f in range(2):
        loads.append(pltpu.make_async_copy(
            tok_in.at[:, pl.ds(f * CH, CH)], tok.at[2 * tp + f], load_sem.at[f]))
    for j, ref in enumerate((wq, wk, wv, wg)):
        loads.append(pltpu.make_async_copy(ref, w.at[j], load_sem.at[2 + j]))
    loads.append(pltpu.make_async_copy(wo, wov, load_sem.at[6]))
    loads.append(pltpu.make_async_copy(st_in, stv, load_sem.at[7]))
    for c in loads:
        c.start()

    barrier = pltpu.get_barrier_semaphore()
    signal(right)
    signal(left)
    signal(partner)
    for d in range(1, NZ):
        signal((y * NZ + (z + d) % NZ, tp))
    for d in range(1, NY):
        signal((((y + d) % NY) * NZ + z, tp))
    pl.semaphore_wait(barrier, 3 + NZ - 1 + NY - 1)

    sends = []

    def go(copy):
        copy.start()
        sends.append(copy)

    def tok_go(n, slot, dev):
        go(remote(tok.at[slot], tok.at[slot], tok_send.at[n], tok_recv.at[slot], dev))

    def tok_wait(slot):
        remote(tok.at[slot], tok.at[slot], tok_send.at[0], tok_recv.at[slot], partner).wait_recv()

    def slot(xx, cc, f):
        return (2 * xx + cc) * 2 + f

    loads[0].wait()
    tok_go(0, slot(x, mine, 0), right)
    tok_go(1, slot(x, mine, 0), partner)
    loads[1].wait()
    tok_go(2, slot(x, mine, 1), left)
    tok_go(3, slot(x, mine, 1), partner)
    tok_go(4, slot(x, mine, 1), right)
    tok_go(5, slot(x, mine, 0), left)

    rates = [rate_ref[2 * tp + h] for h in range(2)]
    pos = lax.broadcasted_iota(jnp.int32, (ROWS, HD), 0).astype(F32)
    gap = (lax.broadcasted_iota(jnp.int32, (HD, ROWS), 0) + (ROWS - HD)
           - lax.broadcasted_iota(jnp.int32, (HD, ROWS), 1))
    lower = gap >= 0
    gap_f = jnp.where(lower, gap, 0).astype(F32)
    for h in range(2):
        tail[h] = jnp.exp(-rates[h] * (ROWS - 1.0 - pos))
        lead[h] = jnp.exp(-rates[h] * (pos + 1.0))
        mask[h] = jnp.where(lower, jnp.exp(-rates[h] * gap_f), 0.0)

    def project(s1, s2, first=False):
        rows1 = pl.ds(pl.multiple_of(s1 * CH, CH), CH)
        rows2 = pl.ds(pl.multiple_of(s2 * CH, CH), CH)

        def body(j, carry):
            part = jnp.dot(tok[s1], w[j, rows1, :], preferred_element_type=F32)
            part += jnp.dot(tok[s2], w[j, rows2, :], preferred_element_type=F32)
            if first:
                acc[j] = part
            else:
                acc[j] += part
            return carry

        lax.fori_loop(0, 4, body, 0)
        a = tok[s1].astype(F32)
        b = tok[s2].astype(F32)
        a = a * a
        b = b * b
        total = (a[:, :HD] + a[:, HD:]) + (b[:, :HD] + b[:, HD:])
        if first:
            sq[...] = total
        else:
            sq[...] += total

    for c in loads[2:6]:
        c.wait()
    project(slot(x, mine, 0), slot(x, mine, 1), True)
    tok_wait(slot(x, other, 0))
    tok_wait(slot(x, other, 1))
    project(slot(x, other, 0), slot(x, other, 1))

    tok_wait(slot(xl, mine, 0))
    tok_go(6, slot(xl, mine, 0), right)
    tok_go(7, slot(xl, mine, 0), partner)
    tok_wait(slot(xr, mine, 1))
    tok_go(8, slot(xr, mine, 1), left)
    tok_go(9, slot(xr, mine, 1), partner)
    project(slot(xl, mine, 0), slot(xr, mine, 1))
    tok_wait(slot(xl, other, 0))
    tok_wait(slot(xr, other, 1))
    project(slot(xl, other, 0), slot(xr, other, 1))

    tok_wait(slot(xl, mine, 1))
    tok_go(10, slot(xl, mine, 1), partner)
    tok_wait(slot(xr, mine, 0))
    tok_go(11, slot(xr, mine, 0), partner)
    project(slot(xl, mine, 1), slot(xr, mine, 0))
    tok_wait(slot(xl, other, 1))
    tok_wait(slot(xr, other, 0))
    project(slot(xl, other, 1), slot(xr, other, 0))

    tok_wait(slot(xo, mine, 0))
    tok_go(12, slot(xo, mine, 0), partner)
    tok_wait(slot(xo, mine, 1))
    tok_go(13, slot(xo, mine, 1), partner)
    project(slot(xo, mine, 0), slot(xo, mine, 1))
    tok_wait(slot(xo, other, 0))
    tok_wait(slot(xo, other, 1))
    project(slot(xo, other, 0), slot(xo, other, 1))

    inv = lax.rsqrt(jnp.sum(sq[...], axis=1, keepdims=True) / float(WIDTH) + 1e-06)
    kb[...] = silu(acc[1] * inv).astype(BF)
    vb[...] = (acc[2] * inv).astype(BF)

    for h in range(2):
        cols = slice(h * HD, (h + 1) * HD)
        scaled = kb[:, cols].astype(F32) * tail[h]
        high = scaled.astype(BF)
        low = (scaled - high.astype(F32)).astype(BF)
        dims = (((0,), (0,)), ((), ()))
        state = lax.dot_general(high, vb[:, cols], dims, preferred_element_type=F32)
        state += lax.dot_general(low, vb[:, cols], dims, preferred_element_type=F32)
        lsend[h * 4:(h + 1) * 4] = state.astype(BF).reshape(4, 32, HD)

    far_first = (4, 3, 5, 2, 6, 1, 7)
    for n, d in enumerate(far_first):
        zz = (z + d) % NZ
        go(remote(lsend.at[zz], r1.at[z], s1s.at[n], s1r.at[z], (y * NZ + zz, tp)))
    r1[z] = lsend[z]

    qb[...] = silu(acc[0] * inv).astype(BF)
    gate[...] = silu(acc[3] * inv)

    def attend(h):
        cols = slice(h * HD, (h + 1) * HD)
        for i in range(4):
            n = (i + 1) * HD
            rows = slice(i * HD, n)
            scores = lax.dot_general(qb[rows, cols], kb[0:n, cols], (((1,), (1,)), ((), ())),
                                     preferred_element_type=F32)
            weights = (scores * mask[h, :, ROWS - n:]).astype(BF)
            intra[rows, cols] = jnp.dot(weights, vb[0:n, cols], preferred_element_type=F32)

    for d in far_first[::-1]:
        zz = (z + d) % NZ
        remote(lsend.at[zz], r1.at[zz], s1s.at[0], s1r.at[zz], partner).wait_recv()
    rate_z = rate_ref[2 * tp + z // 4]
    step = jnp.exp(jnp.full((1, HD), -rate_z * ROWS, F32))
    run = jnp.zeros((32, HD), F32)
    before = []
    for k in range(NZ):
        before.append(run)
        run = step * run + r1[k].astype(F32)
    rtsend[...] = run
    for n, d in enumerate((2, 1, 3)):
        yy = (y + d) % NY
        go(remote(rtsend, rt.at[y], s2s.at[n], s2r.at[y], (yy * NZ + z, tp)))
    rt[y] = run
    attend(0)
    for d in (1, 3, 2):
        yy = (y + d) % NY
        remote(rtsend, rt.at[yy], s2s.at[0], s2r.at[yy], partner).wait_recv()
    start = jnp.zeros((32, HD), F32)
    for k in range(NY):
        gone = jnp.maximum(y - 1 - k, 0).astype(F32) * float(NZ * ROWS)
        factor = jnp.exp(jnp.full((1, HD), -rate_z * gone, F32))
        start += jnp.where(k < y, factor, 0.0) * rt[k]
    for k in range(NZ):
        factor = jnp.exp(jnp.full((1, HD), -rate_z * float(k * ROWS), F32))
        ssend[k] = (before[k] + factor * start).astype(BF)
    for n, d in enumerate(far_first):
        zz = (z + d) % NZ
        go(remote(ssend.at[zz], srecv.at[z], s3s.at[n], s3r.at[z], (y * NZ + zz, tp)))
    srecv[z] = ssend[z]
    attend(1)
    loads[6].wait()
    loads[7].wait()
    for d in far_first[::-1]:
        zz = (z + d) % NZ
        remote(ssend.at[zz], srecv.at[zz], s3s.at[0], s3r.at[zz], partner).wait_recv()
    parts = []
    offset = (ROWS * seq).astype(F32)
    for h in range(2):
        incoming = srecv[h * 4:(h + 1) * 4].astype(F32).reshape(HD, HD)
        incoming += jnp.exp(jnp.full((1, HD), -rates[h] * offset, F32)) * stv[h]
        high = incoming.astype(BF)
        parts.append((high, (incoming - high.astype(F32)).astype(BF)))

    HALF = ROWS // 2

    def hid_go(n, sl, half, dev):
        ref = hid.at[sl, pl.ds(half * HALF, HALF)]
        go(remote(ref, ref, hid_send.at[n], hid_recv.at[2 * sl + half], dev))

    def hid_wait(sl, half):
        ref = hid.at[sl, pl.ds(half * HALF, HALF)]
        remote(ref, ref, hid_send.at[0], hid_recv.at[2 * sl + half], partner).wait_recv()

    for half in range(2):
        rows = slice(half * HALF, (half + 1) * HALF)
        for h in range(2):
            cols = slice(h * HD, (h + 1) * HD)
            q = qb[rows, cols]
            inter = jnp.dot(q, parts[h][0], preferred_element_type=F32)
            inter += jnp.dot(q, parts[h][1], preferred_element_type=F32)
            att = intra[rows, cols] + lead[h, rows, :] * inter
            norm = lax.rsqrt(jnp.mean(att * att, axis=1, keepdims=True) + 1e-06)
            hid[tp, rows, cols] = (att * norm * gate[rows, cols]).astype(BF)
        if half == 0:
            hid_go(0, tp, 0, right)
            hid_go(1, tp, 0, partner)
        else:
            hid_go(2, tp, 1, left)
            hid_go(3, tp, 1, partner)
            hid_go(4, tp, 1, right)
            hid_go(5, tp, 0, left)

    def out_part(sl, half, first=False):
        rows = slice(half * HALF, (half + 1) * HALF)
        part = jnp.dot(hid[sl, rows, :], wov[pl.ds(pl.multiple_of(sl * CH, CH), CH), :],
                       preferred_element_type=F32)
        if first:
            oacc[rows, :] = part
        else:
            oacc[rows, :] += part

    tl, tr, to = 2 * xl, 2 * xr, 2 * xo
    tpp = 2 * x + other
    out_part(tp, 0, True)
    out_part(tp, 1, True)
    hid_wait(tpp, 0)
    out_part(tpp, 0)
    hid_wait(tpp, 1)
    out_part(tpp, 1)

    hid_wait(tl + mine, 0)
    hid_go(6, tl + mine, 0, right)
    hid_go(7, tl + mine, 0, partner)
    hid_wait(tr + mine, 1)
    hid_go(8, tr + mine, 1, left)
    hid_go(9, tr + mine, 1, partner)
    out_part(tl + mine, 0)
    out_part(tr + mine, 1)
    hid_wait(tl + other, 0)
    out_part(tl + other, 0)
    hid_wait(tr + other, 1)
    out_part(tr + other, 1)

    hid_wait(tl + mine, 1)
    hid_go(10, tl + mine, 1, partner)
    hid_wait(tr + mine, 0)
    hid_go(11, tr + mine, 0, partner)
    out_part(tl + mine, 1)
    out_part(tr + mine, 0)
    hid_wait(tl + other, 1)
    out_part(tl + other, 1)
    hid_wait(tr + other, 0)
    out_part(tr + other, 0)

    hid_wait(to + mine, 0)
    hid_go(12, to + mine, 0, partner)
    hid_wait(to + mine, 1)
    hid_go(13, to + mine, 1, partner)
    out_part(to + mine, 0)
    out_part(to + mine, 1)
    hid_wait(to + other, 0)
    out_part(to + other, 0)
    hid_wait(to + other, 1)
    out_part(to + other, 1)

    for f in range(2):
        cols = slice(f * CH, (f + 1) * CH)
        out_ref[:, cols] = (tok[2 * tp + f].astype(F32) + oacc[:, cols]).astype(BF)
    for c in sends:
        c.wait_send()


def per_device(tokens, w_query, w_key, w_value, w_gate, w_out, decay_rate, state_in):
    anyspec = pl.BlockSpec(memory_space=pl.ANY)
    dma = pltpu.SemaphoreType.DMA
    return pl.pallas_call(
        kernel,
        out_shape=jax.ShapeDtypeStruct((ROWS, 512), BF),
        in_specs=[anyspec] * 6 + [pl.BlockSpec(memory_space=pltpu.SMEM), anyspec],
        out_specs=pl.BlockSpec(memory_space=pltpu.VMEM),
        scratch_shapes=[
            pltpu.VMEM((16, ROWS, CH), BF),
            pltpu.VMEM((4, WIDTH, 256), BF),
            pltpu.VMEM((2048, 512), BF),
            pltpu.VMEM((2, HD, HD), F32),
            pltpu.VMEM((4, ROWS, 256), F32),
            pltpu.VMEM((ROWS, HD), F32),
            pltpu.VMEM((2, HD, ROWS), F32),
            pltpu.VMEM((2, ROWS, HD), F32),
            pltpu.VMEM((2, ROWS, HD), F32),
            pltpu.VMEM((ROWS, 256), BF),
            pltpu.VMEM((ROWS, 256), BF),
            pltpu.VMEM((ROWS, 256), BF),
            pltpu.VMEM((ROWS, 256), F32),
            pltpu.VMEM((ROWS, 256), F32),
            pltpu.VMEM((NZ, 32, HD), BF),
            pltpu.VMEM((NZ, 32, HD), BF),
            pltpu.VMEM((32, HD), F32),
            pltpu.VMEM((NY, 32, HD), F32),
            pltpu.VMEM((NZ, 32, HD), BF),
            pltpu.VMEM((NZ, 32, HD), BF),
            pltpu.VMEM((8, ROWS, 256), BF),
            pltpu.VMEM((ROWS, 512), F32),
            dma((8,)), dma((14,)), dma((16,)), dma((7,)), dma((8,)), dma((3,)), dma((4,)),
            dma((7,)), dma((8,)), dma((14,)), dma((16,)),
        ],
        compiler_params=pltpu.CompilerParams(
            collective_id=0, has_side_effects=True, vmem_limit_bytes=56 * 1024 * 1024),
        name="lightning_layer",
    )(tokens, w_query, w_key, w_value, w_gate, w_out, decay_rate, state_in)


def solution(mesh):
    return jax.shard_map(
        per_device,
        mesh=mesh,
        in_specs=(
            P("seq", "tp"),
            P(None, "tp"),
            P(None, "tp"),
            P(None, "tp"),
            P(None, "tp"),
            P(None, "tp"),
            P(),
            P("tp", None, None),
        ),
        out_specs=P("seq", "tp"),
        check_vma=False,
    )
```

time: 187 us -> 61.7 us (0.33)
  waiting for transfers between devices: 135 us -> 0 us
  Pallas kernels: 0 us -> 59.6 us
  matrix products: 26.3 us -> 0 us
  between operations: 13.3 us -> 0.01 us
  other arithmetic: 9.55 us -> 0 us
    all_gather x3 -> x0, waiting for transfers between devices: 135 us -> none  [the longest x1 66.4 us: per_device(): lax.all_gather(local_state[None].astype(jnp.bfloat16), 'seq', axis=0, til...]
    pallas_call x0 -> x1, Pallas kernels: none -> 59.6 us  [per_device(): pl.pallas_call(kernel, out_shape=jax.ShapeDtypeStruct((ROWS, 512), BF), i...]
    dot_general x8 -> x0, matrix products: 26.3 us -> none  [the longest x4 17.1 us: per_device(): jnp.dot(gathered, weight, preferred_element_type=jnp.float32)]
    reduce_sum x2 -> x0, other arithmetic: 5.3 us -> none  [the longest x1 3.23 us: per_device(): square_sum = jnp.sum(gathered_f * gathered_f, axis=1, keepdims=True)]
    exp x2 -> x0, other arithmetic: 1.94 us -> none  [the longest x1 1.26 us: per_device(): incoming = prefix + jnp.exp(-rate_here * offset)[:, None, None] * state_in]
  transfers between devices with their start and end apart: 3 -> 0, of which waited for: 3 -> 0; matrix products, arithmetic and copies ran while one was open for 5% -> 0% of each run, Pallas kernels for 0% -> 0%
where the time goes in v1:
time: 61.7 us; the launch traced here: 61.5 us
  Pallas kernels  59.6 us (97%)
  local copies, waits for them, and re-layouts  1.87 us (3%)
    pallas_call x1, Pallas kernels, per_device(): pl.pallas_call(kernel, out_shape=jax.ShapeDtypeStruct((ROWS, 512), BF), i...  59.6 us
    unnamed x1, local copies, waits for them, and re-layouts  1.87 us

profile of v1, /device:TPU:1, one launch (start us, length us, event | category | flops | bytes accessed | tf_op | source)
XLA Modules:
  0.0 61.5 jit_solution(14604545857819771769)
XLA Ops:
  0.0 59.6 %lightning_layer.1 = bf16[512,512]{1,0:T(8,128)(2,1)} custom-call(bf16[512,512]{1,0:T(8,128)(2,1)} %tok_in.1, bf16[4096,256]{1,0:T(8,128)(2,1)} %wq.1, bf16[4096,256]{1,0:T(8,128)(2,1)} %wk.1, bf16[4096,256]{1,0:T(8,128)(2,1)} %wv.1, bf16[4096,256]{1,0:T(8,128)(2,1)} %wg.1, bf16[2048,512]{1,0:T(8,128)(2,1)} %wo.1, f32[16]{0:T(128)} %rate_ref.1, ...), custom_call_target="tpu_custom_call" | custom-call | tf_op jit(solution)/shard_map/lightning_layer/pallas_call | solution.py:328
  59.7 1.9 %copy.10 = bf16[512,512]{1,0:T(8,128)(2,1)} copy(bf16[512,512]{1,0:T(8,128)(2,1)} %lightning_layer.1) | data formatting | bytes 1048576

commit v2 on v1

--- a/solution.py
+++ b/solution.py
@@ -21,7 +21,7 @@
 def kernel(tok_in, wq, wk, wv, wg, wo, rate_ref, st_in, out_ref,
            tok, w, wov, stv, acc, sq, mask, tail, lead, kb, vb, qb, gate, intra,
            lsend, r1, rtsend, rt, ssend, srecv, hid, oacc,
-           load_sem, tok_send, tok_recv, s1s, s1r, s2s, s2r, s3s, s3r, hid_send, hid_recv):
+           load_sem, tok_send, tok_recv, s1s, s1r, s2s, s2r, s3s, s3r, hid_send, hid_recv, here):
     tp = lax.axis_index("tp")
     seq = lax.axis_index("seq")
     x, core = tp // 2, tp % 2
@@ -51,38 +51,56 @@
         c.start()
 
     barrier = pltpu.get_barrier_semaphore()
-    signal(right)
-    signal(left)
-    signal(partner)
-    for d in range(1, NZ):
-        signal((y * NZ + (z + d) % NZ, tp))
-    for d in range(1, NY):
-        signal((((y + d) % NY) * NZ + z, tp))
-    pl.semaphore_wait(barrier, 3 + NZ - 1 + NY - 1)
-
+    z_up, z_down = (y * NZ + (z + 1) % NZ, tp), (y * NZ + (z + NZ - 1) % NZ, tp)
+    y_up, y_down = (((y + 1) % NY) * NZ + z, tp), (((y + NY - 1) % NY) * NZ + z, tp)
+    for dev in (right, left, partner, z_up, z_down, y_up, y_down):
+        signal(dev)
+    pl.semaphore_wait(barrier, 7)
+
+    def greet(n):
+        for k, dev in enumerate((z_up, z_down) + ((y_up, y_down) if n == 0 else ())):
+            pl.semaphore_signal(here.at[4 * n + k], inc=1, device_id=dev,
+                                device_id_type=pl.DeviceIdType.MESH)
+
+    def greeted(n):
+        for k in range(4 if n == 0 else 2):
+            pl.semaphore_wait(here.at[4 * n + k], 1)
+
+    greet(0)
     sends = []
 
     def go(copy):
         copy.start()
         sends.append(copy)
 
-    def tok_go(n, slot, dev):
-        go(remote(tok.at[slot], tok.at[slot], tok_send.at[n], tok_recv.at[slot], dev))
+    HALF = ROWS // 2
+
+    def tok_copy(n, slot, half, dev):
+        ref = tok.at[slot, pl.ds(half * HALF, HALF)]
+        return remote(ref, ref, tok_send.at[n], tok_recv.at[2 * slot + half], dev)
+
+    def tok_go(slot, half, dev):
+        go(tok_copy(len(sends), slot, half, dev))
 
     def tok_wait(slot):
-        remote(tok.at[slot], tok.at[slot], tok_send.at[0], tok_recv.at[slot], partner).wait_recv()
+        for half in range(2):
+            tok_copy(0, slot, half, partner).wait_recv()
 
     def slot(xx, cc, f):
         return (2 * xx + cc) * 2 + f
 
     loads[0].wait()
-    tok_go(0, slot(x, mine, 0), right)
-    tok_go(1, slot(x, mine, 0), partner)
+    for half in range(2):
+        tok_go(slot(x, mine, 0), half, right)
     loads[1].wait()
-    tok_go(2, slot(x, mine, 1), left)
-    tok_go(3, slot(x, mine, 1), partner)
-    tok_go(4, slot(x, mine, 1), right)
-    tok_go(5, slot(x, mine, 0), left)
+    for half in range(2):
+        tok_go(slot(x, mine, 1), half, left)
+    for f in range(2):
+        for half in range(2):
+            tok_go(slot(x, mine, f), half, partner)
+    for half in range(2):
+        tok_go(slot(x, mine, 1), half, right)
+        tok_go(slot(x, mine, 0), half, left)
 
     rates = [rate_ref[2 * tp + h] for h in range(2)]
     pos = lax.broadcasted_iota(jnp.int32, (ROWS, HD), 0).astype(F32)
@@ -119,41 +137,46 @@
         else:
             sq[...] += total
 
+    def pass_on(s_left, s_right, forward):
+        for half in range(2):
+            tok_copy(0, s_left, half, partner).wait_recv()
+            if forward:
+                tok_go(s_left, half, right)
+            tok_go(s_left, half, partner)
+            tok_copy(0, s_right, half, partner).wait_recv()
+            if forward:
+                tok_go(s_right, half, left)
+            tok_go(s_right, half, partner)
+
     for c in loads[2:6]:
         c.wait()
     project(slot(x, mine, 0), slot(x, mine, 1), True)
+    greeted(0)
+    greet(1)
     tok_wait(slot(x, other, 0))
     tok_wait(slot(x, other, 1))
     project(slot(x, other, 0), slot(x, other, 1))
 
-    tok_wait(slot(xl, mine, 0))
-    tok_go(6, slot(xl, mine, 0), right)
-    tok_go(7, slot(xl, mine, 0), partner)
-    tok_wait(slot(xr, mine, 1))
-    tok_go(8, slot(xr, mine, 1), left)
-    tok_go(9, slot(xr, mine, 1), partner)
+    pass_on(slot(xl, mine, 0), slot(xr, mine, 1), True)
     project(slot(xl, mine, 0), slot(xr, mine, 1))
+    greeted(1)
+    greet(2)
     tok_wait(slot(xl, other, 0))
     tok_wait(slot(xr, other, 1))
     project(slot(xl, other, 0), slot(xr, other, 1))
 
-    tok_wait(slot(xl, mine, 1))
-    tok_go(10, slot(xl, mine, 1), partner)
-    tok_wait(slot(xr, mine, 0))
-    tok_go(11, slot(xr, mine, 0), partner)
+    pass_on(slot(xl, mine, 1), slot(xr, mine, 0), False)
     project(slot(xl, mine, 1), slot(xr, mine, 0))
     tok_wait(slot(xl, other, 1))
     tok_wait(slot(xr, other, 0))
     project(slot(xl, other, 1), slot(xr, other, 0))
 
-    tok_wait(slot(xo, mine, 0))
-    tok_go(12, slot(xo, mine, 0), partner)
-    tok_wait(slot(xo, mine, 1))
-    tok_go(13, slot(xo, mine, 1), partner)
+    pass_on(slot(xo, mine, 0), slot(xo, mine, 1), False)
     project(slot(xo, mine, 0), slot(xo, mine, 1))
     tok_wait(slot(xo, other, 0))
     tok_wait(slot(xo, other, 1))
     project(slot(xo, other, 0), slot(xo, other, 1))
+    greeted(2)
 
     inv = lax.rsqrt(jnp.sum(sq[...], axis=1, keepdims=True) / float(WIDTH) + 1e-06)
     kb[...] = silu(acc[1] * inv).astype(BF)
@@ -233,8 +256,6 @@
         high = incoming.astype(BF)
         parts.append((high, (incoming - high.astype(F32)).astype(BF)))
 
-    HALF = ROWS // 2
-
     def hid_go(n, sl, half, dev):
         ref = hid.at[sl, pl.ds(half * HALF, HALF)]
         go(remote(ref, ref, hid_send.at[n], hid_recv.at[2 * sl + half], dev))
@@ -353,8 +374,9 @@
             pltpu.VMEM((NZ, 32, HD), BF),
             pltpu.VMEM((8, ROWS, 256), BF),
             pltpu.VMEM((ROWS, 512), F32),
-            dma((8,)), dma((14,)), dma((16,)), dma((7,)), dma((8,)), dma((3,)), dma((4,)),
+            dma((8,)), dma((28,)), dma((32,)), dma((7,)), dma((8,)), dma((3,)), dma((4,)),
             dma((7,)), dma((8,)), dma((14,)), dma((16,)),
+            pltpu.SemaphoreType.REGULAR((10,)),
         ],
         compiler_params=pltpu.CompilerParams(
             collective_id=0, has_side_effects=True, vmem_limit_bytes=56 * 1024 * 1024),

time: 61.7 us -> 59.6 us (0.966)
  Pallas kernels: 59.6 us -> 57.6 us
    pallas_call x1, Pallas kernels: 59.6 us -> 57.6 us  [per_device(): pl.pallas_call(kernel, out_shape=jax.ShapeDtypeStruct((ROWS, 512), BF), i...]
where the time goes in v2:
time: 59.6 us; the launch traced here: 59.5 us
  Pallas kernels  57.6 us (97%)
  local copies, waits for them, and re-layouts  1.87 us (3%)
    pallas_call x1, Pallas kernels, per_device(): pl.pallas_call(kernel, out_shape=jax.ShapeDtypeStruct((ROWS, 512), BF), i...  57.6 us
    unnamed x1, local copies, waits for them, and re-layouts  1.87 us

profile of v2, /device:TPU:1, one launch (start us, length us, event | category | flops | bytes accessed | tf_op | source)
XLA Modules:
  0.0 59.5 jit_solution(5818893060477713544)
XLA Ops:
  0.0 57.6 %lightning_layer.1 = bf16[512,512]{1,0:T(8,128)(2,1)} custom-call(bf16[512,512]{1,0:T(8,128)(2,1)} %tok_in.1, bf16[4096,256]{1,0:T(8,128)(2,1)} %wq.1, bf16[4096,256]{1,0:T(8,128)(2,1)} %wk.1, bf16[4096,256]{1,0:T(8,128)(2,1)} %wv.1, bf16[4096,256]{1,0:T(8,128)(2,1)} %wg.1, bf16[2048,512]{1,0:T(8,128)(2,1)} %wo.1, f32[16]{0:T(128)} %rate_ref.1, ...), custom_call_target="tpu_custom_call" | custom-call | tf_op jit(solution)/shard_map/lightning_layer/pallas_call | solution.py:349
  57.7 1.9 %copy.10 = bf16[512,512]{1,0:T(8,128)(2,1)} copy(bf16[512,512]{1,0:T(8,128)(2,1)} %lightning_layer.1) | data formatting | bytes 1048576

commit v3 on v2

--- a/solution.py
+++ b/solution.py
@@ -113,7 +113,7 @@
         lead[h] = jnp.exp(-rates[h] * (pos + 1.0))
         mask[h] = jnp.where(lower, jnp.exp(-rates[h] * gap_f), 0.0)
 
-    def project(s1, s2, first=False):
+    def project(s1, s2, first=False, lo=0, hi=4, squares=True):
         rows1 = pl.ds(pl.multiple_of(s1 * CH, CH), CH)
         rows2 = pl.ds(pl.multiple_of(s2 * CH, CH), CH)
 
@@ -126,7 +126,9 @@
                 acc[j] += part
             return carry
 
-        lax.fori_loop(0, 4, body, 0)
+        lax.fori_loop(lo, hi, body, 0)
+        if not squares:
+            return
         a = tok[s1].astype(F32)
         b = tok[s2].astype(F32)
         a = a * a
@@ -175,7 +177,8 @@
     project(slot(xo, mine, 0), slot(xo, mine, 1))
     tok_wait(slot(xo, other, 0))
     tok_wait(slot(xo, other, 1))
-    project(slot(xo, other, 0), slot(xo, other, 1))
+    last = (slot(xo, other, 0), slot(xo, other, 1))
+    project(*last, lo=1, hi=3)
     greeted(2)
 
     inv = lax.rsqrt(jnp.sum(sq[...], axis=1, keepdims=True) / float(WIDTH) + 1e-06)
@@ -184,12 +187,9 @@
 
     for h in range(2):
         cols = slice(h * HD, (h + 1) * HD)
-        scaled = kb[:, cols].astype(F32) * tail[h]
-        high = scaled.astype(BF)
-        low = (scaled - high.astype(F32)).astype(BF)
-        dims = (((0,), (0,)), ((), ()))
-        state = lax.dot_general(high, vb[:, cols], dims, preferred_element_type=F32)
-        state += lax.dot_general(low, vb[:, cols], dims, preferred_element_type=F32)
+        scaled = (kb[:, cols].astype(F32) * tail[h]).astype(BF)
+        state = lax.dot_general(scaled, vb[:, cols], (((0,), (0,)), ((), ())),
+                                preferred_element_type=F32)
         lsend[h * 4:(h + 1) * 4] = state.astype(BF).reshape(4, 32, HD)
 
     far_first = (4, 3, 5, 2, 6, 1, 7)
@@ -198,8 +198,8 @@
         go(remote(lsend.at[zz], r1.at[z], s1s.at[n], s1r.at[z], (y * NZ + zz, tp)))
     r1[z] = lsend[z]
 
+    project(*last, lo=0, hi=1, squares=False)
     qb[...] = silu(acc[0] * inv).astype(BF)
-    gate[...] = silu(acc[3] * inv)
 
     def attend(h):
         cols = slice(h * HD, (h + 1) * HD)
@@ -211,6 +211,7 @@
             weights = (scores * mask[h, :, ROWS - n:]).astype(BF)
             intra[rows, cols] = jnp.dot(weights, vb[0:n, cols], preferred_element_type=F32)
 
+    attend(0)
     for d in far_first[::-1]:
         zz = (z + d) % NZ
         remote(lsend.at[zz], r1.at[zz], s1s.at[0], s1r.at[zz], partner).wait_recv()
@@ -226,7 +227,7 @@
         yy = (y + d) % NY
         go(remote(rtsend, rt.at[y], s2s.at[n], s2r.at[y], (yy * NZ + z, tp)))
     rt[y] = run
-    attend(0)
+    attend(1)
     for d in (1, 3, 2):
         yy = (y + d) % NY
         remote(rtsend, rt.at[yy], s2s.at[0], s2r.at[yy], partner).wait_recv()
@@ -242,7 +243,8 @@
         zz = (z + d) % NZ
         go(remote(ssend.at[zz], srecv.at[z], s3s.at[n], s3r.at[z], (y * NZ + zz, tp)))
     srecv[z] = ssend[z]
-    attend(1)
+    project(*last, lo=3, hi=4, squares=False)
+    gate[...] = silu(acc[3] * inv)
     loads[6].wait()
     loads[7].wait()
     for d in far_first[::-1]:
@@ -256,16 +258,22 @@
         high = incoming.astype(BF)
         parts.append((high, (incoming - high.astype(F32)).astype(BF)))
 
-    def hid_go(n, sl, half, dev):
-        ref = hid.at[sl, pl.ds(half * HALF, HALF)]
-        go(remote(ref, ref, hid_send.at[n], hid_recv.at[2 * sl + half], dev))
-
-    def hid_wait(sl, half):
-        ref = hid.at[sl, pl.ds(half * HALF, HALF)]
-        remote(ref, ref, hid_send.at[0], hid_recv.at[2 * sl + half], partner).wait_recv()
-
-    for half in range(2):
-        rows = slice(half * HALF, (half + 1) * HALF)
+    QUARTER = ROWS // 4
+    first_hid = len(sends)
+
+    def hid_copy(n, sl, part, dev):
+        ref = hid.at[sl, pl.ds(part * QUARTER, QUARTER)]
+        return remote(ref, ref, hid_send.at[n], hid_recv.at[4 * sl + part], dev)
+
+    def hid_go(sl, part, *devs):
+        for dev in devs:
+            go(hid_copy(len(sends) - first_hid, sl, part, dev))
+
+    def hid_wait(sl, part):
+        hid_copy(0, sl, part, partner).wait_recv()
+
+    for part in (0, 2, 1, 3):
+        rows = slice(part * QUARTER, (part + 1) * QUARTER)
         for h in range(2):
             cols = slice(h * HD, (h + 1) * HD)
             q = qb[rows, cols]
@@ -274,14 +282,10 @@
             att = intra[rows, cols] + lead[h, rows, :] * inter
             norm = lax.rsqrt(jnp.mean(att * att, axis=1, keepdims=True) + 1e-06)
             hid[tp, rows, cols] = (att * norm * gate[rows, cols]).astype(BF)
-        if half == 0:
-            hid_go(0, tp, 0, right)
-            hid_go(1, tp, 0, partner)
-        else:
-            hid_go(2, tp, 1, left)
-            hid_go(3, tp, 1, partner)
-            hid_go(4, tp, 1, right)
-            hid_go(5, tp, 0, left)
+        hid_go(tp, part, right if part < 2 else left, partner)
+    for i in range(2):
+        hid_go(tp, 2 + i, right)
+        hid_go(tp, i, left)
 
     def out_part(sl, half, first=False):
         rows = slice(half * HALF, (half + 1) * HALF)
@@ -292,49 +296,47 @@
         else:
             oacc[rows, :] += part
 
+    def arrived(sl, half):
+        hid_wait(sl, 2 * half)
+        hid_wait(sl, 2 * half + 1)
+        out_part(sl, half)
+
     tl, tr, to = 2 * xl, 2 * xr, 2 * xo
     tpp = 2 * x + other
     out_part(tp, 0, True)
     out_part(tp, 1, True)
-    hid_wait(tpp, 0)
-    out_part(tpp, 0)
-    hid_wait(tpp, 1)
-    out_part(tpp, 1)
-
-    hid_wait(tl + mine, 0)
-    hid_go(6, tl + mine, 0, right)
-    hid_go(7, tl + mine, 0, partner)
-    hid_wait(tr + mine, 1)
-    hid_go(8, tr + mine, 1, left)
-    hid_go(9, tr + mine, 1, partner)
+    arrived(tpp, 0)
+    arrived(tpp, 1)
+
+    for i in range(2):
+        hid_wait(tl + mine, i)
+        hid_go(tl + mine, i, right, partner)
+        hid_wait(tr + mine, 2 + i)
+        hid_go(tr + mine, 2 + i, left, partner)
     out_part(tl + mine, 0)
     out_part(tr + mine, 1)
-    hid_wait(tl + other, 0)
-    out_part(tl + other, 0)
-    hid_wait(tr + other, 1)
-    out_part(tr + other, 1)
-
-    hid_wait(tl + mine, 1)
-    hid_go(10, tl + mine, 1, partner)
-    hid_wait(tr + mine, 0)
-    hid_go(11, tr + mine, 0, partner)
+    arrived(tl + other, 0)
+    arrived(tr + other, 1)
+
+    for i in range(2):
+        hid_wait(tl + mine, 2 + i)
+        hid_go(tl + mine, 2 + i, partner)
+        hid_wait(tr + mine, i)
+        hid_go(tr + mine, i, partner)
     out_part(tl + mine, 1)
     out_part(tr + mine, 0)
-    hid_wait(tl + other, 1)
-    out_part(tl + other, 1)
-    hid_wait(tr + other, 0)
-    out_part(tr + other, 0)
-
-    hid_wait(to + mine, 0)
-    hid_go(12, to + mine, 0, partner)
-    hid_wait(to + mine, 1)
-    hid_go(13, to + mine, 1, partner)
+    arrived(tl + other, 1)
+    arrived(tr + other, 0)
+
+    for i in range(2):
+        hid_wait(to + mine, i)
+        hid_go(to + mine, i, partner)
+        hid_wait(to + mine, 2 + i)
+        hid_go(to + mine, 2 + i, partner)
     out_part(to + mine, 0)
     out_part(to + mine, 1)
-    hid_wait(to + other, 0)
-    out_part(to + other, 0)
-    hid_wait(to + other, 1)
-    out_part(to + other, 1)
+    arrived(to + other, 0)
+    arrived(to + other, 1)
 
     for f in range(2):
         cols = slice(f * CH, (f + 1) * CH)
@@ -375,7 +377,7 @@
             pltpu.VMEM((8, ROWS, 256), BF),
             pltpu.VMEM((ROWS, 512), F32),
             dma((8,)), dma((28,)), dma((32,)), dma((7,)), dma((8,)), dma((3,)), dma((4,)),
-            dma((7,)), dma((8,)), dma((14,)), dma((16,)),
+            dma((7,)), dma((8,)), dma((28,)), dma((32,)),
             pltpu.SemaphoreType.REGULAR((10,)),
         ],
         compiler_params=pltpu.CompilerParams(

time: 59.6 us -> 58.9 us (0.988)
  Pallas kernels: 57.6 us -> 56.9 us
    pallas_call x1, Pallas kernels: 57.6 us -> 56.9 us  [per_device(): pl.pallas_call(kernel, out_shape=jax.ShapeDtypeStruct((ROWS, 512), BF), i...]
where the time goes in v3:
time: 58.9 us; the launch traced here: 58.8 us
  Pallas kernels  56.9 us (97%)
  local copies, waits for them, and re-layouts  1.87 us (3%)
    pallas_call x1, Pallas kernels, per_device(): pl.pallas_call(kernel, out_shape=jax.ShapeDtypeStruct((ROWS, 512), BF), i...  56.9 us
    unnamed x1, local copies, waits for them, and re-layouts  1.87 us

profile of v3, /device:TPU:1, one launch (start us, length us, event | category | flops | bytes accessed | tf_op | source)
XLA Modules:
  0.0 58.8 jit_solution(9855256201808430642)
XLA Ops:
  0.0 56.9 %lightning_layer.1 = bf16[512,512]{1,0:T(8,128)(2,1)} custom-call(bf16[512,512]{1,0:T(8,128)(2,1)} %tok_in.1, bf16[4096,256]{1,0:T(8,128)(2,1)} %wq.1, bf16[4096,256]{1,0:T(8,128)(2,1)} %wk.1, bf16[4096,256]{1,0:T(8,128)(2,1)} %wv.1, bf16[4096,256]{1,0:T(8,128)(2,1)} %wg.1, bf16[2048,512]{1,0:T(8,128)(2,1)} %wo.1, f32[16]{0:T(128)} %rate_ref.1, ...), custom_call_target="tpu_custom_call" | custom-call | tf_op jit(solution)/shard_map/lightning_layer/pallas_call | solution.py:351
  56.9 1.9 %copy.10 = bf16[512,512]{1,0:T(8,128)(2,1)} copy(bf16[512,512]{1,0:T(8,128)(2,1)} %lightning_layer.1) | data formatting | bytes 1048576

commit v4 on v3

--- a/solution.py
+++ b/solution.py
@@ -350,7 +350,7 @@
     dma = pltpu.SemaphoreType.DMA
     return pl.pallas_call(
         kernel,
-        out_shape=jax.ShapeDtypeStruct((ROWS, 512), BF),
+        out_shape=pltpu.VMEM((ROWS, 512), BF),
         in_specs=[anyspec] * 6 + [pl.BlockSpec(memory_space=pltpu.SMEM), anyspec],
         out_specs=pl.BlockSpec(memory_space=pltpu.VMEM),
         scratch_shapes=[

time: 58.9 us -> 57 us (0.968)
  local copies, waits for them, and re-layouts: 1.87 us -> 0.8 us
  Pallas kernels: 56.9 us -> 56.1 us
    unnamed x1, local copies, waits for them, and re-layouts: 1.87 us -> 0.8 us
    pallas_call x1, Pallas kernels: 56.9 us -> 56.1 us  [per_device(): pl.pallas_call(kernel, out_shape=pltpu.VMEM((ROWS, 512), BF), in_specs=[a...]
where the time goes in v4:
time: 57 us; the launch traced here: 56.9 us
  Pallas kernels  56.1 us (98%)
  local copies, waits for them, and re-layouts  0.8 us (1%)
    pallas_call x1, Pallas kernels, per_device(): pl.pallas_call(kernel, out_shape=pltpu.VMEM((ROWS, 512), BF), in_specs=[a...  56.1 us

profile of v4, /device:TPU:1, one launch (start us, length us, event | category | flops | bytes accessed | tf_op | source)
XLA Modules:
  0.0 56.9 jit_solution(13664617831576924685)
XLA Ops:
  0.0 56.1 %lightning_layer.1 = bf16[512,512]{1,0:T(8,128)(2,1)S(1)} custom-call(bf16[512,512]{1,0:T(8,128)(2,1)} %tok_in.1, bf16[4096,256]{1,0:T(8,128)(2,1)} %wq.1, bf16[4096,256]{1,0:T(8,128)(2,1)} %wk.1, bf16[4096,256]{1,0:T(8,128)(2,1)} %wv.1, bf16[4096,256]{1,0:T(8,128)(2,1)} %wg.1, bf16[2048,512]{1,0:T(8,128)(2,1)} %wo.1, f32[16]{0:T(128)} %rate_ref.1, ...), custom_call_target="tpu_custom_call" | custom-call | tf_op jit(solution)/shard_map/lightning_layer/pallas_call | solution.py:351
  56.1 0.8 %copy.10 = bf16[512,512]{1,0:T(8,128)(2,1)} copy(bf16[512,512]{1,0:T(8,128)(2,1)S(1)} %lightning_layer.1) | data formatting | bytes 1048576

commit v5 on v4

--- a/solution.py
+++ b/solution.py
@@ -113,31 +113,31 @@
         lead[h] = jnp.exp(-rates[h] * (pos + 1.0))
         mask[h] = jnp.where(lower, jnp.exp(-rates[h] * gap_f), 0.0)
 
-    def project(s1, s2, first=False, lo=0, hi=4, squares=True):
+    def project(s1, s2, first=False, lo=0, hi=4, squares=True, r=slice(0, ROWS)):
         rows1 = pl.ds(pl.multiple_of(s1 * CH, CH), CH)
         rows2 = pl.ds(pl.multiple_of(s2 * CH, CH), CH)
 
         def body(j, carry):
-            part = jnp.dot(tok[s1], w[j, rows1, :], preferred_element_type=F32)
-            part += jnp.dot(tok[s2], w[j, rows2, :], preferred_element_type=F32)
+            part = jnp.dot(tok[s1, r, :], w[j, rows1, :], preferred_element_type=F32)
+            part += jnp.dot(tok[s2, r, :], w[j, rows2, :], preferred_element_type=F32)
             if first:
-                acc[j] = part
+                acc[j, r, :] = part
             else:
-                acc[j] += part
+                acc[j, r, :] += part
             return carry
 
         lax.fori_loop(lo, hi, body, 0)
         if not squares:
             return
-        a = tok[s1].astype(F32)
-        b = tok[s2].astype(F32)
+        a = tok[s1, r, :].astype(F32)
+        b = tok[s2, r, :].astype(F32)
         a = a * a
         b = b * b
         total = (a[:, :HD] + a[:, HD:]) + (b[:, :HD] + b[:, HD:])
         if first:
-            sq[...] = total
+            sq[r, :] = total
         else:
-            sq[...] += total
+            sq[r, :] += total
 
     def pass_on(s_left, s_right, forward):
         for half in range(2):
@@ -173,12 +173,16 @@
     tok_wait(slot(xr, other, 0))
     project(slot(xl, other, 1), slot(xr, other, 0))
 
-    pass_on(slot(xo, mine, 0), slot(xo, mine, 1), False)
-    project(slot(xo, mine, 0), slot(xo, mine, 1))
-    tok_wait(slot(xo, other, 0))
-    tok_wait(slot(xo, other, 1))
-    last = (slot(xo, other, 0), slot(xo, other, 1))
-    project(*last, lo=1, hi=3)
+    last = [(slot(xo, c, 0), slot(xo, c, 1)) for c in (mine, other)]
+    for half in range(2):
+        r = slice(half * HALF, (half + 1) * HALF)
+        for sl in last[0]:
+            tok_copy(0, sl, half, partner).wait_recv()
+            tok_go(sl, half, partner)
+        project(*last[0], lo=1, hi=3, r=r)
+        for sl in last[1]:
+            tok_copy(0, sl, half, partner).wait_recv()
+        project(*last[1], lo=1, hi=3, r=r)
     greeted(2)
 
     inv = lax.rsqrt(jnp.sum(sq[...], axis=1, keepdims=True) / float(WIDTH) + 1e-06)
@@ -198,7 +202,8 @@
         go(remote(lsend.at[zz], r1.at[z], s1s.at[n], s1r.at[z], (y * NZ + zz, tp)))
     r1[z] = lsend[z]
 
-    project(*last, lo=0, hi=1, squares=False)
+    for pair in last:
+        project(*pair, lo=0, hi=1, squares=False)
     qb[...] = silu(acc[0] * inv).astype(BF)
 
     def attend(h):
@@ -243,7 +248,8 @@
         zz = (z + d) % NZ
         go(remote(ssend.at[zz], srecv.at[z], s3s.at[n], s3r.at[z], (y * NZ + zz, tp)))
     srecv[z] = ssend[z]
-    project(*last, lo=3, hi=4, squares=False)
+    for pair in last:
+        project(*pair, lo=3, hi=4, squares=False)
     gate[...] = silu(acc[3] * inv)
     loads[6].wait()
     loads[7].wait()

time: 57 us -> 57 us (level)
  no operation moved by 1% of the time
where the time goes in v5:
time: 57 us; the launch traced here: 56.9 us
  Pallas kernels  56.1 us (98%)
  local copies, waits for them, and re-layouts  0.8 us (1%)
    pallas_call x1, Pallas kernels, per_device(): pl.pallas_call(kernel, out_shape=pltpu.VMEM((ROWS, 512), BF), in_specs=[a...  56.1 us

profile of v5, /device:TPU:1, one launch (start us, length us, event | category | flops | bytes accessed | tf_op | source)
XLA Modules:
  0.0 56.9 jit_solution(9922524618613769580)
XLA Ops:
  0.0 56.1 %lightning_layer.1 = bf16[512,512]{1,0:T(8,128)(2,1)S(1)} custom-call(bf16[512,512]{1,0:T(8,128)(2,1)} %tok_in.1, bf16[4096,256]{1,0:T(8,128)(2,1)} %wq.1, bf16[4096,256]{1,0:T(8,128)(2,1)} %wk.1, bf16[4096,256]{1,0:T(8,128)(2,1)} %wv.1, bf16[4096,256]{1,0:T(8,128)(2,1)} %wg.1, bf16[2048,512]{1,0:T(8,128)(2,1)} %wo.1, f32[16]{0:T(128)} %rate_ref.1, ...), custom_call_target="tpu_custom_call" | custom-call | tf_op jit(solution)/shard_map/lightning_layer/pallas_call | solution.py:357
  56.1 0.8 %copy.10 = bf16[512,512]{1,0:T(8,128)(2,1)} copy(bf16[512,512]{1,0:T(8,128)(2,1)S(1)} %lightning_layer.1) | data formatting | bytes 1048576

commit v6 on v4

--- a/solution.py
+++ b/solution.py
@@ -227,7 +227,6 @@
         yy = (y + d) % NY
         go(remote(rtsend, rt.at[y], s2s.at[n], s2r.at[y], (yy * NZ + z, tp)))
     rt[y] = run
-    attend(1)
     for d in (1, 3, 2):
         yy = (y + d) % NY
         remote(rtsend, rt.at[yy], s2s.at[0], s2r.at[yy], partner).wait_recv()
@@ -244,6 +243,7 @@
         go(remote(ssend.at[zz], srecv.at[z], s3s.at[n], s3r.at[z], (y * NZ + zz, tp)))
     srecv[z] = ssend[z]
     project(*last, lo=3, hi=4, squares=False)
+    attend(1)
     gate[...] = silu(acc[3] * inv)
     loads[6].wait()
     loads[7].wait()

time: 57 us -> 57 us (level)
  no operation moved by 1% of the time
where the time goes in v6:
time: 57 us; the launch traced here: 56.9 us
  Pallas kernels  56.1 us (98%)
  local copies, waits for them, and re-layouts  0.8 us (1%)
    pallas_call x1, Pallas kernels, per_device(): pl.pallas_call(kernel, out_shape=pltpu.VMEM((ROWS, 512), BF), in_specs=[a...  56.1 us

profile of v6, /device:TPU:1, one launch (start us, length us, event | category | flops | bytes accessed | tf_op | source)
XLA Modules:
  0.0 56.9 jit_solution(7283925950852871401)
XLA Ops:
  0.0 56.1 %lightning_layer.1 = bf16[512,512]{1,0:T(8,128)(2,1)S(1)} custom-call(bf16[512,512]{1,0:T(8,128)(2,1)} %tok_in.1, bf16[4096,256]{1,0:T(8,128)(2,1)} %wq.1, bf16[4096,256]{1,0:T(8,128)(2,1)} %wk.1, bf16[4096,256]{1,0:T(8,128)(2,1)} %wv.1, bf16[4096,256]{1,0:T(8,128)(2,1)} %wg.1, bf16[2048,512]{1,0:T(8,128)(2,1)} %wo.1, f32[16]{0:T(128)} %rate_ref.1, ...), custom_call_target="tpu_custom_call" | custom-call | tf_op jit(solution)/shard_map/lightning_layer/pallas_call | solution.py:351
  56.1 0.8 %copy.10 = bf16[512,512]{1,0:T(8,128)(2,1)} copy(bf16[512,512]{1,0:T(8,128)(2,1)S(1)} %lightning_layer.1) | data formatting | bytes 1048576
